TPU v7x, 32 devices: a whole 2x2x4 slice. The times are simulated.
32 devices in a mesh: frame: 8 (over y, x, core), head: 4 (over z).
Axes of the slice: x: 2, y: 2, z: 4, core: 2. Of those that a mesh axis runs over, the one named last changes fastest.
Arguments:
- queries: bfloat16 [4, 2048, 4096], P(None, 'frame', 'head'), may hold values from -6 to 6
- keys: bfloat16 [4, 2048, 4096], P(None, 'frame', 'head'), may hold values from -6 to 6
- values: bfloat16 [4, 2048, 4096], P(None, 'frame', 'head'), may hold values from -6 to 6
- step_sizes: bfloat16 [4, 2048, 16], P(None, 'frame', 'head'), may hold values from 9e-05 to 1.25, as said below
- starts: int32 [4], replicated, may hold values from 0 to 7, as said below
- resets: int32 [4, 8], replicated, may hold values 0 or 1
- init_in: bfloat16 [16, 256, 1024], P('head'), may hold values from -0.375 to 0.375
- init_out: bfloat16 [16, 512, 256], P('head'), may hold values from -0.25 to 0.25
- gain: float32 [4096], P('head'), may hold values from 0.25 to 1.75
- out_proj: bfloat16 [4096, 5120], P('head'), may hold values from -0.125 to 0.125
Outputs:
- mixed_out: bfloat16 [4, 2048, 5120], P(None, 'frame', 'head')
Inputs may be any that keep to these rules, and one draw needn't show every extreme that they name: `starts`: 4 distinct blocks. `step_sizes`: positive.
All inputs are finite; a program needn't handle non-finite values.
Results may differ from a plain program's by a relative error of at most 0.035.
Values may be sent and summed in bfloat16 or wider, within the bound.
No kernel may reach another device: no remote copies, remote signals or barrier semaphores. Data moves between devices by JAX's collectives and lax.ppermute only.
A program may use at most 128 MiB of HBM per device.

v0:
```python
import jax
import jax.numpy as jnp
from jax import lax
from jax.sharding import PartitionSpec as P


def renorm(raw_weights, target):
    column_scale = target[:, None, :] * lax.rsqrt(
        jnp.sum(raw_weights * raw_weights, axis=1, keepdims=True) + 1e-06
    )
    return (raw_weights * column_scale).astype(jnp.bfloat16)


def advance(
    weights_in, weights_out, queries_seg, keys_seg, values_seg, rates_seg, norm_in, norm_out, gain
):
    rows_here = queries_seg.shape[0]
    heads_here = weights_in.shape[0]
    head_width = weights_in.shape[1]
    hidden_width = weights_out.shape[1]
    key_heads = keys_seg.reshape(rows_here, heads_here, head_width)
    pre_keys = jnp.einsum("thd,hde->hte", key_heads, weights_in, preferred_element_type=jnp.float32)
    first_half = pre_keys[..., :hidden_width]
    second_half = pre_keys[..., hidden_width:]
    sigmoid_first = jax.nn.sigmoid(first_half)
    activated = first_half * sigmoid_first
    hidden = (activated * second_half).astype(jnp.bfloat16)
    value_heads = values_seg.reshape(rows_here, heads_here, head_width).astype(jnp.float32)
    scaled = (value_heads * rates_seg.astype(jnp.float32)[:, :, None]).astype(jnp.bfloat16)
    grad_hidden = jnp.einsum(
        "the,hfe->htf", scaled, weights_out, preferred_element_type=jnp.float32
    )
    grad_first = (
        grad_hidden * second_half * sigmoid_first * (1.0 + first_half * (1.0 - sigmoid_first))
    )
    grad_second = grad_hidden * activated
    grad_pre = jnp.concatenate([grad_first, grad_second], axis=-1).astype(jnp.bfloat16)
    raw_in = weights_in.astype(jnp.float32) + jnp.einsum(
        "thd,hte->hde", key_heads, grad_pre, preferred_element_type=jnp.float32
    )
    raw_out = weights_out.astype(jnp.float32) + jnp.einsum(
        "htf,the->hfe", hidden, scaled, preferred_element_type=jnp.float32
    )
    new_in = renorm(raw_in, norm_in)
    new_out = renorm(raw_out, norm_out)
    query_heads = queries_seg.reshape(rows_here, heads_here, head_width)
    pre_queries = jnp.einsum(
        "thd,hde->hte", query_heads, new_in, preferred_element_type=jnp.float32
    )
    hidden_queries = (
        jax.nn.silu(pre_queries[..., :hidden_width]) * pre_queries[..., hidden_width:]
    ).astype(jnp.bfloat16)
    fast_out = jnp.einsum(
        "htf,hfe->the", hidden_queries, new_out, preferred_element_type=jnp.float32
    )
    normed = fast_out * lax.rsqrt(jnp.mean(fast_out * fast_out, axis=-1, keepdims=True) + 1e-05)
    normed = normed * gain.reshape(heads_here, head_width)
    return (
        new_in,
        new_out,
        normed.reshape(rows_here, heads_here * head_width).astype(jnp.bfloat16),
    )


def shards(queries, keys, values, step_sizes, starts, resets, init_in, init_out, gain, out_proj):
    frames = lax.axis_size("frame")
    position = lax.axis_index("frame")
    videos = queries.shape[0]
    rows_block = queries.shape[1]
    norm_in = jnp.sqrt(jnp.sum(jnp.square(init_in.astype(jnp.float32)), axis=1))
    norm_out = jnp.sqrt(jnp.sum(jnp.square(init_out.astype(jnp.float32)), axis=1))
    padding = ((0, frames - videos), (0, 0), (0, 0))
    moved_queries, moved_keys, moved_values, moved_rates = (
        lax.all_to_all(jnp.pad(queries, padding), "frame", split_axis=0, concat_axis=1, tiled=True),
        lax.all_to_all(jnp.pad(keys, padding), "frame", split_axis=0, concat_axis=1, tiled=True),
        lax.all_to_all(jnp.pad(values, padding), "frame", split_axis=0, concat_axis=1, tiled=True),
        lax.all_to_all(
            jnp.pad(step_sizes, padding), "frame", split_axis=0, concat_axis=1, tiled=True
        ),
    )
    video_here = jnp.minimum(position, videos - 1)
    first_block = starts[video_here]
    reset_flags = resets[video_here]

    def local_segment(seg_index, loop_state):
        state_in, state_out, collected = loop_state
        block_now = (first_block + seg_index) % frames
        first_row = block_now * rows_block
        queries_seg = lax.dynamic_slice_in_dim(moved_queries[0], first_row, rows_block, 0)
        keys_seg = lax.dynamic_slice_in_dim(moved_keys[0], first_row, rows_block, 0)
        values_seg = lax.dynamic_slice_in_dim(moved_values[0], first_row, rows_block, 0)
        rates_seg = lax.dynamic_slice_in_dim(moved_rates[0], first_row, rows_block, 0)
        restart = jnp.logical_or(seg_index == 0, reset_flags[seg_index] == 1)
        weights_in = jnp.where(restart, init_in, state_in)
        weights_out = jnp.where(restart, init_out, state_out)
        new_in, new_out, normed = advance(
            weights_in,
            weights_out,
            queries_seg,
            keys_seg,
            values_seg,
            rates_seg,
            norm_in,
            norm_out,
            gain,
        )
        collected = lax.dynamic_update_slice_in_dim(collected, normed, first_row, 0)
        return (new_in, new_out, collected)

    empty_rows = jnp.zeros((moved_queries.shape[1], moved_queries.shape[2]), jnp.bfloat16)
    _, _, own_rows = lax.fori_loop(0, frames, local_segment, (init_in, init_out, empty_rows))
    returned = lax.all_to_all(own_rows[None], "frame", split_axis=1, concat_axis=0, tiled=True)
    normed_all = returned[:videos]
    flat_rows = normed_all.reshape(videos * rows_block, normed_all.shape[2])
    partial_value = jnp.dot(flat_rows, out_proj, preferred_element_type=jnp.float32)
    mixed_out = lax.psum_scatter(
        partial_value.astype(jnp.bfloat16), "head", scatter_dimension=1, tiled=True
    ).astype(jnp.float32)
    return mixed_out.astype(jnp.bfloat16).reshape(videos, rows_block, mixed_out.shape[1])


def solution(mesh):
    return jax.shard_map(
        shards,
        mesh=mesh,
        in_specs=(
            P(None, "frame", "head"),
            P(None, "frame", "head"),
            P(None, "frame", "head"),
            P(None, "frame", "head"),
            P(),
            P(),
            P("head", None, None),
            P("head", None, None),
            P("head"),
            P("head", None),
        ),
        out_specs=P(None, "frame", "head"),
        check_vma=False,
    )
```

profile of v0, /device:TPU:0, one launch (start us, length us, event | category | flops | bytes accessed | tf_op | source)
XLA Modules:
  0.0 668.5 jit_solution(5543504575499884247)
XLA Ops:
  6.5 1.3 pad.16
  7.9 5.2 all-to-all-start.2
  13.1 4.1 pad.17
  17.8 4.6 all-to-all-start.3
  22.4 2.5 pad.14
  24.9 46.6 %all-to-all-done.3 = bf16[8,256,1024]{2,1,0:T(8,128)(2,1)} async-done(((bf16[8,256,1024]{2,1,0:T(8,128)(2,1)}), bf16[8,256,1024]{2,1,0:T(8,128)(2,1)}, u32[]{:S(2)}, u32[]{:S(2)}) %all-to-all-start.3) | async-done | bytes 4194336 | tf_op jit(solution)/shard_map/all_to_all | solution.py:74
  71.5 4.6 all-to-all-start
  76.1 2.4 pad.15
  78.5 46.7 %all-to-all-done = bf16[8,256,1024]{2,1,0:T(8,128)(2,1)} async-done(((bf16[8,256,1024]{2,1,0:T(8,128)(2,1)}), bf16[8,256,1024]{2,1,0:T(8,128)(2,1)}, u32[]{:S(2)}, u32[]{:S(2)}) %all-to-all-start) | async-done | bytes 4194336 | tf_op jit(solution)/shard_map/all_to_all | solution.py:75
  125.1 4.6 all-to-all-start.1
  131.1 1.7 copy.77
  134.6 44.3 %all-to-all-done.1 = bf16[8,256,1024]{2,1,0:T(8,128)(2,1)} async-done(((bf16[8,256,1024]{2,1,0:T(8,128)(2,1)}), bf16[8,256,1024]{2,1,0:T(8,128)(2,1)}, u32[]{:S(2)}, u32[]{:S(2)}) %all-to-all-start.1) | async-done | bytes 4194336 | tf_op jit(solution)/shard_map/all_to_all | solution.py:76
  178.8 2.5 broadcast_in_dim.24
  181.3 163.1 %while.20 = (s32[]{:T(128)}, bf16[4,256,1024]{2,1,0:T(8,128)(2,1)S(1)}, bf16[4,512,256]{2,1,0:T(8,128)(2,1)}, bf16[2048,1024]{0,1:T(8,128)(2,1)}, s32[8]{0:T(128...) while((s32[]{:T(128)}, ...), condition=%wide.wide.region_6.7_spmd, body=%wide.wide.region_2.6_spmd.sunk | while | flops 2449480704 | bytes 95033920 | solution.py:111
  183.3 1.1 constant_dynamic-slice_fusion.4
  184.5 2.4 dynamic-slice_convert_fusion.3
  186.9 2.7 reshape.137
  190.6 1.9 broadcast_select_fusion.5
  194.4 1.6 multiply_convert_fusion.15
  195.9 1.4 multiply_reduce_fusion.12
  204.4 1.1 constant_dynamic-slice_fusion.4
  205.7 2.4 dynamic-slice_convert_fusion.3
  208.1 2.7 reshape.137
  211.8 1.9 broadcast_select_fusion.5
  215.6 1.5 multiply_convert_fusion.15
  217.1 1.4 multiply_reduce_fusion.12
  226.9 2.4 dynamic-slice_convert_fusion.3
  229.3 2.7 reshape.137
  235.2 1.6 multiply_convert_fusion.15
  236.7 1.4 multiply_reduce_fusion.12
  245.2 1.1 constant_dynamic-slice_fusion.4
  246.5 2.4 dynamic-slice_convert_fusion.3
  248.9 2.7 reshape.137
  252.6 1.9 broadcast_select_fusion.5
  256.4 1.6 multiply_convert_fusion.15
  257.9 1.4 multiply_reduce_fusion.12
  267.7 2.4 dynamic-slice_convert_fusion.3
  270.1 2.7 reshape.137
  276.0 1.6 multiply_convert_fusion.15
  277.5 1.4 multiply_reduce_fusion.12
  286.0 1.1 constant_dynamic-slice_fusion.4
  287.3 2.4 dynamic-slice_convert_fusion.3
  289.7 2.7 reshape.137
  295.6 1.5 multiply_convert_fusion.15
  297.1 1.4 multiply_reduce_fusion.12
  305.6 1.1 constant_dynamic-slice_fusion.4
  306.9 2.4 dynamic-slice_convert_fusion.3
  309.2 2.7 reshape.137
  312.9 1.9 broadcast_select_fusion.5
  316.7 1.6 multiply_convert_fusion.15
  318.3 1.4 multiply_reduce_fusion.12
  326.8 1.1 constant_dynamic-slice_fusion.4
  328.1 2.4 dynamic-slice_convert_fusion.3
  330.4 2.7 reshape.137
  336.3 1.6 multiply_convert_fusion.15
  337.9 1.4 multiply_reduce_fusion.12
  344.4 20.5 %copy.42 = bf16[1,2048,1024]{2,0,1:T(2,128)(2,1)} copy(bf16[1,2048,1024]{1,2,0:T(8,128)(2,1)} %bitcast.69) | data formatting | bytes 8388608 | tf_op jit(solution)/shard_map/broadcast_in_dim | solution.py:112
  365.5 26.0 %reduce = bf16[2048,1024]{1,0:T(8,128)(2,1)} reduce(bf16[2048,1,1024]{2,1,0:T(2,128)(2,1)} %bitcast.67, bf16[]{:T(256)} %broadcast.99), dimensions={1}, to_apply=%bitcast.20.reduce_sub_computation | reduce | bytes 8388610
  391.4 7.8 %reshape.133 = bf16[8,2,131072]{2,1,0:T(2,128)(2,1)} reshape(bf16[2048,1024]{1,0:T(8,128)(2,1)} %reduce) | data formatting | bytes 8388608
  399.2 53.6 %all_to_all.60 = bf16[8,2,131072]{2,1,0:T(2,128)(2,1)} all-to-all(bf16[8,2,131072]{2,1,0:T(2,128)(2,1)} %reshape.133), channel_id=1, replica_groups=mesh['frame'=8,'head'=4] {'frame'}, dimensions={0} | all-to-all | bytes 8388608 | tf_op jit(solution)/shard_map/all_to_all | solution.py:112
  452.8 8.8 %reshape.134 = bf16[2048,1,1024]{2,1,0:T(2,128)(2,1)} reshape(bf16[8,2,131072]{2,1,0:T(2,128)(2,1)} %all_to_all.60) | data formatting | bytes 8388608
  461.5 5.1 copy.53
  466.8 17.2 %convolution_convert_fusion = bf16[1024,5120]{1,0:T(8,128)(2,1)} fusion(bf16[1024,1024]{1,0:T(8,128)(2,1)S(1)} %bitcast.71, bf16[1024,5120]{1,0:T(8,128)(2,1)} %param.21), kind=kOutput, calls=%fused_computation.36 | convolution fusion | flops 10742661120 | bytes 23068672 | tf_op jit(solution)/shard_map/dot_general | solution.py:115
  484.1 177.5 %reduce-scatter.2.cloned.1.call-done = bf16[1024,1280]{1,0:T(8,128)(2,1)} async-done(((bf16[1024,5120]{1,0:T(8,128)(2,1)}), bf16[1024,1280]{1,0:T(8,128)(2,1)}) %reduce-scatter.2.cloned.1.call-update) | async-done | bytes 2621456 | tf_op jit(solution)/shard_map/reduce_scatter | solution.py:116
  (235 shorter events, 77.4 us)
Async XLA Ops:
  6.5 128.0 %copy-start = (s32[4,8]{1,0:T(4,128)S(1)}, s32[4,8]{1,0:T(4,128)}, u32[]{:S(2)}) copy-start(s32[4,8]{1,0:T(4,128)} %param.17) | copy-start | bytes 388
  7.9 10.0 %all-to-all-start.2 = ((bf16[8,256,4]{1,2,0:T(4,128)(2,1)}), bf16[8,256,4]{1,2,0:T(4,128)(2,1)S(1)}, u32[]{:S(2)}, u32[]{:S(2)}) async-start(bf16[8,256,4]{1,2,0:T(4,128)(2,1)} %pad.16), calls=%async_computation.2 | async-start | bytes 32768 | tf_op jit(solution)/shard_map/all_to_all | solution.py:77
  17.1 5.3 copy-start.7
  17.8 53.7 %all-to-all-start.3 = ((bf16[8,256,1024]{2,1,0:T(8,128)(2,1)}), bf16[8,256,1024]{2,1,0:T(8,128)(2,1)}, u32[]{:S(2)}, u32[]{:S(2)}) async-start(bf16[8,256,1024]{2,1,0:T(8,128)(2,1)} %pad.17), calls=%async_computation.3 | async-start | bytes 8388608 | tf_op jit(solution)/shard_map/all_to_all | solution.py:74
  24.9 51.2 %copy-start.8 = (bf16[4,256,1024]{2,1,0:T(8,128)(2,1)S(1)}, bf16[4,256,1024]{2,1,0:T(8,128)(2,1)}, u32[]{:S(2)}) copy-start(bf16[4,256,1024]{2,1,0:T(8,128)(2,1)} %param.14) | copy-start | bytes 6291460
  71.5 53.7 %all-to-all-start = ((bf16[8,256,1024]{2,1,0:T(8,128)(2,1)}), bf16[8,256,1024]{2,1,0:T(8,128)(2,1)}, u32[]{:S(2)}, u32[]{:S(2)}) async-start(bf16[8,256,1024]{2,1,0:T(8,128)(2,1)} %pad.14), calls=%async_computation | async-start | bytes 8388608 | tf_op jit(solution)/shard_map/all_to_all | solution.py:75
  78.5 51.3 %copy-start.11 = (f32[1024]{0:T(1024)S(1)}, f32[1024]{0:T(1024)}, u32[]{:S(2)}) copy-start(f32[1024]{0:T(1024)} %param.20) | copy-start | bytes 12292
  78.5 51.3 %copy-start.5 = (bf16[4,512,256]{2,1,0:T(8,128)(2,1)S(1)}, bf16[4,512,256]{2,1,0:T(8,128)(2,1)}, u32[]{:S(2)}) copy-start(bf16[4,512,256]{2,1,0:T(8,128)(2,1)} %param.19) | copy-start | bytes 3145732
  125.1 53.7 %all-to-all-start.1 = ((bf16[8,256,1024]{2,1,0:T(8,128)(2,1)}), bf16[8,256,1024]{2,1,0:T(8,128)(2,1)}, u32[]{:S(2)}, u32[]{:S(2)}) async-start(bf16[8,256,1024]{2,1,0:T(8,128)(2,1)} %pad.15), calls=%async_computation.1 | async-start | bytes 8388608 | tf_op jit(solution)/shard_map/all_to_all | solution.py:76
  129.7 531.9 %reduce-scatter.2.cloned.1.call-start = ((), (), s32[]{:S(2)}) async-start(), calls=%async_computation.6 | async-start | bytes 13107200 | tf_op jit(solution)/shard_map/reduce_scatter | solution.py:116
  131.0 2.2 copy-start.2
  133.3 0.7 copy-start.12
  192.5 1.2 copy-start.4
  192.5 1.5 copy-start.6
  192.5 1.8 copy-start.9
  197.6 2.8 copy-start.10
  198.6 1.0 copy-start.3
  213.7 1.2 copy-start.4
  213.7 1.5 copy-start.6
  213.7 1.8 copy-start.9
  218.8 2.8 copy-start.10
  219.8 1.0 copy-start.3
  233.3 1.2 copy-start.4
  233.3 1.5 copy-start.6
  233.3 1.8 copy-start.9
  238.4 2.8 copy-start.10
  239.4 1.0 copy-start.3
  254.5 1.2 copy-start.4
  254.5 1.5 copy-start.6
  254.5 1.8 copy-start.9
  259.6 2.8 copy-start.10
  260.6 1.0 copy-start.3
  274.1 1.2 copy-start.4
  274.1 1.5 copy-start.6
  274.1 1.8 copy-start.9
  279.2 2.8 copy-start.10
  280.2 1.0 copy-start.3
  293.7 1.2 copy-start.4
  293.7 1.5 copy-start.6
  293.7 1.8 copy-start.9
  298.8 2.8 copy-start.10
  299.8 1.0 copy-start.3
  314.9 1.2 copy-start.4
  314.9 1.5 copy-start.6
  314.9 1.8 copy-start.9
  319.9 2.8 copy-start.10
  320.9 1.0 copy-start.3
  334.5 1.2 copy-start.4
  334.5 1.5 copy-start.6
  334.5 1.8 copy-start.9
  339.5 2.8 copy-start.10
  340.5 1.0 copy-start.3
  484.1 177.6 %copy-start.1 = (s32[4,8]{1,0:T(4,128)S(1)}, s32[4,8]{1,0:T(4,128)}, u32[]{:S(2)}) copy-start(s32[4,8]{1,0:T(4,128)} %param.17) | copy-start | bytes 388
Sparse Core Ops, SparseCore 0:
  484.2 177.3 reduce-scatter.1
where the time goes:
time: 672 us; the launch traced here: 668 us
  waiting for transfers between devices  316 us (47%)
  local copies, waits for them, and re-layouts  122 us (18%)
  matrix products  68.7 us (10%)
  other arithmetic  64.2 us (10%)
  blocking collectives  53.6 us (8%)
  starting transfers between devices  19 us (3%)
  between operations  13.5 us (2%)
  loops' own time  11.9 us (2%)
    reduce_scatter x1, waiting for transfers between devices, shards(): lax.psum_scatter(partial_value.astype(jnp.bfloat16), 'head', scatter_dime...  178 us
    all_to_all x1, blocking collectives, shards(): lax.all_to_all(own_rows[None], 'frame', split_axis=1, concat_axis=0, tile...  53.6 us
    all_to_all x1, waiting for transfers between devices, shards(): lax.all_to_all(jnp.pad(keys, padding), 'frame', split_axis=0, concat_axis...  46.7 us
    all_to_all x1, waiting for transfers between devices, shards(): lax.all_to_all(jnp.pad(queries, padding), 'frame', split_axis=0, concat_a...  46.6 us
    all_to_all x1, waiting for transfers between devices, shards(): lax.all_to_all(jnp.pad(values, padding), 'frame', split_axis=0, concat_ax...  44.3 us
    unnamed x1, other arithmetic  26 us
    unnamed x22, local copies, waits for them, and re-layouts  25.5 us
    convert_element_type x8, local copies, waits for them, and re-layouts, advance(): values_seg.reshape(rows_here, heads_here, head_width).astype(jnp.float32)  21.3 us
  transfers between devices with their start and end apart: 5, of which 5 were waited for; matrix products, arithmetic and copies ran while one was open for 2% of the time, Pallas kernels for 0%

commit v1 on v0

v1 whole, which is shorter than its diff:
```python
import functools

import jax
import jax.numpy as jnp
from jax import lax
from jax.experimental import pallas as pl
from jax.experimental.pallas import tpu as pltpu
from jax.sharding import PartitionSpec as P


def dot(left, right, left_dim, right_dim):
    return lax.dot_general(
        left,
        right,
        (((left_dim,), (right_dim,)), ((), ())),
        preferred_element_type=jnp.float32,
    )


def sigmoid(x):
    return 0.5 + 0.5 * jnp.tanh(0.5 * x)


def renorm(raw, target):
    scale = target * lax.rsqrt(jnp.sum(raw * raw, axis=0, keepdims=True) + 1e-06)
    return (raw * scale).astype(jnp.bfloat16)


def column_norm(weights):
    wide = weights.astype(jnp.float32)
    return jnp.sqrt(jnp.sum(wide * wide, axis=0, keepdims=True))


def chain_kernel(
    plan_ref, rows_ref, init_in_ref, init_out_ref, gain_ref, out_ref, w_in, w_out, norm_in, norm_out
):
    seg = pl.program_id(0)
    hidden_width = w_out.shape[0]

    @pl.when(seg == 0)
    def _():
        norm_in[...] = column_norm(init_in_ref[0])
        norm_out[...] = column_norm(init_out_ref[0])

    @pl.when(jnp.logical_or(seg == 0, plan_ref[2 + seg] == 1))
    def _():
        w_in[...] = init_in_ref[0]
        w_out[...] = init_out_ref[0]

    queries, keys, scaled = rows_ref[0, 0], rows_ref[0, 1], rows_ref[0, 2]
    pre = dot(keys, w_in[...], 1, 0)
    first, second = pre[:, :hidden_width], pre[:, hidden_width:]
    gate = sigmoid(first)
    act = first * gate
    hidden = (act * second).astype(jnp.bfloat16)
    grad_hidden = dot(scaled, w_out[...], 1, 1)
    grad_first = (grad_hidden * second * (gate + act * (1.0 - gate))).astype(jnp.bfloat16)
    grad_second = (grad_hidden * act).astype(jnp.bfloat16)
    grad_pre = jnp.concatenate([grad_first, grad_second], axis=1)
    new_in = renorm(w_in[...].astype(jnp.float32) + dot(keys, grad_pre, 0, 0), norm_in[...])
    new_out = renorm(w_out[...].astype(jnp.float32) + dot(hidden, scaled, 0, 0), norm_out[...])
    w_in[...] = new_in
    w_out[...] = new_out
    pre_q = dot(queries, new_in, 1, 0)
    first_q = pre_q[:, :hidden_width]
    hidden_q = (first_q * sigmoid(first_q) * pre_q[:, hidden_width:]).astype(jnp.bfloat16)
    fast = dot(hidden_q, new_out, 1, 0)
    spread = lax.rsqrt(jnp.mean(fast * fast, axis=1, keepdims=True) + 1e-05)
    out_ref[0] = (fast * spread * gain_ref[0]).astype(jnp.bfloat16)


def run_chain(plan, moved, init_in, init_out, gain):
    segs, _, rows, width = moved.shape
    wide, hidden_width = init_in.shape[2], init_out.shape[1]
    heads = gain.shape[0]
    turn = lambda s, plan: lax.rem(plan[0] + s, segs)
    flops = segs * rows * width * (wide * 3 + hidden_width * 3) * 2
    return pl.pallas_call(
        chain_kernel,
        out_shape=jax.ShapeDtypeStruct((segs, rows, width), jnp.bfloat16),
        grid_spec=pltpu.PrefetchScalarGridSpec(
            num_scalar_prefetch=1,
            grid=(segs,),
            in_specs=[
                pl.BlockSpec((1, 3, rows, width), lambda s, plan: (turn(s, plan), 0, 0, 0)),
                pl.BlockSpec((1, width, wide), lambda s, plan: (plan[1], 0, 0)),
                pl.BlockSpec((1, hidden_width, width), lambda s, plan: (plan[1], 0, 0)),
                pl.BlockSpec((1, 1, width), lambda s, plan: (plan[1], 0, 0)),
            ],
            out_specs=pl.BlockSpec((1, rows, width), lambda s, plan: (turn(s, plan), 0, 0)),
            scratch_shapes=[
                pltpu.VMEM((width, wide), jnp.bfloat16),
                pltpu.VMEM((hidden_width, width), jnp.bfloat16),
                pltpu.VMEM((1, wide), jnp.float32),
                pltpu.VMEM((1, width), jnp.float32),
            ],
        ),
        cost_estimate=pl.CostEstimate(
            flops=flops, bytes_accessed=2 * (moved.size + segs * rows * width), transcendentals=0
        ),
        name="chain",
    )(plan, moved, init_in, init_out, gain.reshape(heads, 1, width))


def shards(queries, keys, values, step_sizes, starts, resets, init_in, init_out, gain, out_proj):
    frames = lax.axis_size("frame")
    place = lax.axis_index("frame")
    videos, rows, _ = queries.shape
    heads, width, _ = init_in.shape
    per_set = max(1, min(videos, frames // heads))
    gain_heads = gain.reshape(heads, width)
    scaled = (
        values.reshape(videos, rows, heads, width).astype(jnp.float32)
        * step_sizes.astype(jnp.float32)[..., None]
    ).astype(jnp.bfloat16)
    head_here = lax.rem(place, heads)
    spread = []
    for first in range(0, videos, per_set):
        pick = lambda x: (
            x[first : first + per_set]
            .reshape(per_set, rows, heads, width)
            .transpose(0, 2, 1, 3)
            .reshape(per_set * heads, rows, width)
        )
        packed = jnp.stack([pick(queries), pick(keys), pick(scaled)], axis=1)
        packed = jnp.pad(packed, ((0, frames - per_set * heads), (0, 0), (0, 0), (0, 0)))
        spread.append(lax.all_to_all(packed, "frame", split_axis=0, concat_axis=0, tiled=True))
    normed = []
    for index, moved in enumerate(spread):
        video = index * per_set + jnp.minimum(place // heads, per_set - 1)
        plan = jnp.concatenate([starts[video][None], head_here[None], resets[video]])
        own = run_chain(plan.astype(jnp.int32), moved, init_in, init_out, gain_heads)
        back = lax.all_to_all(own, "frame", split_axis=0, concat_axis=0, tiled=True)
        normed.append(
            back[: per_set * heads]
            .reshape(per_set, heads, rows, width)
            .transpose(0, 2, 1, 3)
            .reshape(per_set * rows, heads * width)
        )
    parts = []
    for flat in normed:
        partial = jnp.dot(flat, out_proj, preferred_element_type=jnp.float32)
        parts.append(
            lax.psum_scatter(
                partial.astype(jnp.bfloat16), "head", scatter_dimension=1, tiled=True
            )
        )
    mixed = jnp.concatenate(parts, axis=0)
    return mixed.reshape(videos, rows, mixed.shape[1])


def solution(mesh):
    blocks = P(None, "frame", "head")
    return jax.shard_map(
        shards,
        mesh=mesh,
        in_specs=(
            blocks,
            blocks,
            blocks,
            blocks,
            P(),
            P(),
            P("head", None, None),
            P("head", None, None),
            P("head"),
            P("head", None),
        ),
        out_specs=blocks,
        check_vma=False,
    )
```

time: 672 us -> 306 us (0.46)
  waiting for transfers between devices: 316 us -> 172 us
  local copies, waits for them, and re-layouts: 122 us -> 7.86 us
  other arithmetic: 64.2 us -> 12.6 us
  matrix products: 68.7 us -> 22.6 us
  Pallas kernels: 0 us -> 29.9 us
  blocking collectives: 53.6 us -> 37.6 us
  loops' own time: 11.9 us -> 0 us
  starting transfers between devices: 19 us -> 9.06 us
    reduce_scatter x1 -> x2, waiting for transfers between devices: 178 us -> 99.2 us  [shards(): lax.psum_scatter(partial.astype(jnp.bfloat16), 'head', scatter_dimension=...]
    all_to_all x4 -> x2, waiting for transfers between devices: 138 us -> 72.6 us  [shards(): lax.all_to_all(packed, 'frame', split_axis=0, concat_axis=0, tiled=True)]
    dot_general x49 -> x2, matrix products: 68.7 us -> 22.6 us  [shards(): partial = jnp.dot(flat, out_proj, preferred_element_type=jnp.float32)]
    pallas_call x0 -> x2, Pallas kernels: none -> 29.9 us  [run_chain(): pl.pallas_call(chain_kernel, out_shape=jax.ShapeDtypeStruct((segs, rows,...]
    unnamed x1 -> x0, other arithmetic: 26 us -> none
    convert_element_type x40 -> x3, other arithmetic: 28.2 us -> 2.78 us  [the longest x1 2.05 us: shards(): values.reshape(videos, rows, heads, width).astype(jnp.float32)]
    dynamic_slice x33 -> x1, local copies, waits for them, and re-layouts: 23.9 us -> 0.59 us  [shards(): starts[video][None]]
    broadcast_in_dim x2 -> x0, local copies, waits for them, and re-layouts: 23 us -> none  [the longest x1 20.5 us: shards(): own_rows[None]]
  transfers between devices with their start and end apart: 5 -> 4, of which waited for: 5 -> 4; matrix products, arithmetic and copies ran while one was open for 2% -> 6% of each run, Pallas kernels for 0% -> 5%
where the time goes in v1:
time: 306 us; the launch traced here: 305 us
  waiting for transfers between devices  172 us (56%)
  blocking collectives  37.6 us (12%)
  Pallas kernels  29.9 us (10%)
  matrix products  22.6 us (7%)
  between operations  13.6 us (4%)
  other arithmetic  12.6 us (4%)
  starting transfers between devices  9.06 us (3%)
  local copies, waits for them, and re-layouts  7.86 us (3%)
    reduce_scatter x2, waiting for transfers between devices, shards(): lax.psum_scatter(partial.astype(jnp.bfloat16), 'head', scatter_dimension=...  99.2 us
    all_to_all x2, waiting for transfers between devices, shards(): lax.all_to_all(packed, 'frame', split_axis=0, concat_axis=0, tiled=True)  72.6 us
    all_to_all x2, blocking collectives, shards(): back = lax.all_to_all(own, 'frame', split_axis=0, concat_axis=0, tiled=True)  37.6 us
    pallas_call x2, Pallas kernels, run_chain(): pl.pallas_call(chain_kernel, out_shape=jax.ShapeDtypeStruct((segs, rows,...  29.9 us
    dot_general x2, matrix products, shards(): partial = jnp.dot(flat, out_proj, preferred_element_type=jnp.float32)  22.6 us
    all_to_all x2, starting transfers between devices, shards(): lax.all_to_all(packed, 'frame', split_axis=0, concat_axis=0, tiled=True)  8.98 us
  transfers between devices with their start and end apart: 4, of which 4 were waited for; matrix products, arithmetic and copies ran while one was open for 6% of the time, Pallas kernels for 5%

profile of v1, /device:TPU:0, one launch (start us, length us, event | category | flops | bytes accessed | tf_op | source)
XLA Modules:
  0.0 305.0 jit_solution(8285023691120862313)
XLA Ops:
  6.5 0.0 copy-start.3
  6.5 2.1 convert_element_type.24
  8.6 0.0 copy-done.3
  8.6 0.7 fusion
  9.3 0.0 copy-start.1
  9.4 0.2 fusion.3
  9.6 1.4 copy-done.1
  10.9 0.0 copy-start.2
  10.9 0.2 fusion.1
  11.1 0.1 copy.38
  11.2 1.3 copy-done.2
  12.5 0.2 fusion.2
  12.7 0.1 copy.37
  12.8 2.0 pad_maximum_fusion
  14.8 0.0 copy-start.4
  14.8 0.0 copy-start.5
  14.8 5.3 %all-to-all-start = ((bf16[8,3,256,256]{3,2,1,0:T(8,128)(2,1)}), bf16[8,3,256,256]{3,2,1,0:T(8,128)(2,1)}, u32[]{:S(2)}, u32[]{:S(2)}) async-start(bf16[8,3,256,256]{3,2,1,0:T(8,128)(2,1)} %pad_maximum_fusion), calls=%async_computation | async-start | bytes 6291456 | tf_op jit(solution)/shard_map/all_to_all | solution.py:127
  20.1 0.0 reduce-scatter.3.cloned.1.call-start
  20.2 0.0 copy-done.4
  20.2 0.6 fusion.4
  20.8 0.0 copy-done.5
  20.8 1.3 pad_add_fusion.plan_ref
  22.1 36.0 %all-to-all-done.rows_ref = bf16[8,3,256,256]{3,2,1,0:T(8,128)(2,1)} async-done(((bf16[8,3,256,256]{3,2,1,0:T(8,128)(2,1)}), bf16[8,3,256,256]{3,2,1,0:T(8,128)(2,1)}, u32[]{:S(2)}, u32[]{:S(2)}) %all-to-all-start) | async-done | bytes 3145760 | tf_op jit(solution)/shard_map/all_to_all | solution.py:127
  58.1 14.9 %chain.2 = bf16[8,256,256]{2,1,0:T(8,128)(2,1)} custom-call(s32[10]{0:T(128)} %pad_add_fusion.plan_ref, bf16[8,3,256,256]{3,2,1,0:T(8,128)(2,1)} %all-to-all-done.rows_ref, bf16[4,256,1024]{2,1,0:T(8,128)(2,1)} %init_in_ref.3, bf16[4,512,256]{2,1,0:T(8,128)(2,1)} %init_out_ref.3, f32[4,1,256]{2,1,0:T(1,128)} %bitcast.77), custom_call_target="tpu_custom_call" | custom-call | flops 4831838208 | bytes 4194304 | tf_op jit(solution)/shard_map/chain/pallas_call | solution.py:78
  73.0 18.8 %all_to_all.20 = bf16[8,256,256]{2,1,0:T(8,128)(2,1)S(1)} all-to-all(bf16[8,256,256]{2,1,0:T(8,128)(2,1)} %chain.2), channel_id=1, replica_groups=mesh['frame'=8,'head'=4] {'frame'}, dimensions={0} | all-to-all | bytes 2097152 | tf_op jit(solution)/shard_map/all_to_all | solution.py:133
  91.8 0.8 copy.19
  92.6 0.2 copy.28
  92.8 11.3 %convolution_convert_fusion.1 = bf16[512,5120]{1,0:T(8,128)(2,1)} fusion(bf16[512,1024]{1,0:T(8,128)(2,1)S(1)} %bitcast.75, bf16[1024,5120]{1,0:T(8,128)(2,1)} %param.19), kind=kOutput, calls=%fused_computation.1 | convolution fusion | flops 5371330560 | bytes 16777216 | tf_op jit(solution)/shard_map/dot_general | solution.py:142
  104.1 0.0 reduce-scatter.3.cloned.1.call-update
  104.2 0.1 copy.36
  104.2 0.1 copy.35
  104.3 2.0 pad_maximum_fusion.1
  106.3 3.6 %all-to-all-start.2 = ((bf16[8,3,256,256]{3,2,1,0:T(8,128)(2,1)}), bf16[8,3,256,256]{3,2,1,0:T(8,128)(2,1)S(1)}, u32[]{:S(2)}, u32[]{:S(2)}) async-start(bf16[8,3,256,256]{3,2,1,0:T(8,128)(2,1)} %pad_maximum_fusion.1), calls=%async_computation.3 | async-start | bytes 6291456 | tf_op jit(solution)/shard_map/all_to_all | solution.py:127
  110.0 0.0 reduce-scatter.5.cloned.1.call-start
  110.0 1.2 pad_add_fusion.1.plan_ref
  111.2 36.6 %all-to-all-done.2.rows_ref = bf16[8,3,256,256]{3,2,1,0:T(8,128)(2,1)S(1)} async-done(((bf16[8,3,256,256]{3,2,1,0:T(8,128)(2,1)}), bf16[8,3,256,256]{3,2,1,0:T(8,128)(2,1)S(1)}, u32[]{:S(2)}, u32[]{:S(2)}) %all-to-all-start.2) | async-done | bytes 3145760 | tf_op jit(solution)/shard_map/all_to_all | solution.py:127
  147.7 0.0 copy-start
  147.8 1.6 copy-done
  149.4 15.0 %chain.3 = bf16[8,256,256]{2,1,0:T(8,128)(2,1)} custom-call(s32[10]{0:T(128)} %pad_add_fusion.1.plan_ref, bf16[8,3,256,256]{3,2,1,0:T(8,128)(2,1)} %copy-done, bf16[4,256,1024]{2,1,0:T(8,128)(2,1)} %init_in_ref.3, bf16[4,512,256]{2,1,0:T(8,128)(2,1)} %init_out_ref.3, f32[4,1,256]{2,1,0:T(1,128)} %bitcast.78), custom_call_target="tpu_custom_call" | custom-call | flops 4831838208 | bytes 4194304 | tf_op jit(solution)/shard_map/chain/pallas_call | solution.py:78
  164.4 18.8 %all_to_all.21 = bf16[8,256,256]{2,1,0:T(8,128)(2,1)S(1)} all-to-all(bf16[8,256,256]{2,1,0:T(8,128)(2,1)} %chain.3), channel_id=1, replica_groups=mesh['frame'=8,'head'=4] {'frame'}, dimensions={0} | all-to-all | bytes 2097152 | tf_op jit(solution)/shard_map/all_to_all | solution.py:133
  183.2 0.8 copy.22
  184.0 0.2 copy.29
  184.2 11.3 %convolution_convert_fusion = bf16[512,5120]{1,0:T(8,128)(2,1)} fusion(bf16[512,1024]{1,0:T(8,128)(2,1)S(1)} %bitcast.76, bf16[1024,5120]{1,0:T(8,128)(2,1)} %param.19), kind=kOutput, calls=%fused_computation | convolution fusion | flops 5371330560 | bytes 16777216 | tf_op jit(solution)/shard_map/dot_general | solution.py:142
  195.6 0.0 reduce-scatter.5.cloned.1.call-update
  195.6 2.5 reduce-scatter.3.cloned.1.call-done
  198.1 96.7 %reduce-scatter.5.cloned.1.call-done = bf16[512,1280]{1,0:T(8,128)(2,1)} async-done(((bf16[512,5120]{1,0:T(8,128)(2,1)}), bf16[512,1280]{1,0:T(8,128)(2,1)}) %reduce-scatter.5.cloned.1.call-update) | async-done | bytes 1310736 | tf_op jit(solution)/shard_map/reduce_scatter | solution.py:144
  294.8 3.4 %pad_maximum_fusion.2 = bf16[1024,1280]{1,0:T(8,128)(2,1)} fusion(bf16[512,1280]{1,0:T(8,128)(2,1)} %reduce-scatter.5.cloned.1.call-done, bf16[512,1280]{1,0:T(8,128)(2,1)} %reduce-scatter.3.cloned.1.call-done), kind=kLoop, calls=%fused_computation.6 | loop fusion | flops 5242880 | bytes 5242880 | tf_op jit(solution)/shard_map/concatenate | solution.py:148
  (2 shorter events, 0.0 us)
Async XLA Ops:
  6.5 2.1 copy-start.3
  9.3 1.6 copy-start.1
  10.9 1.6 copy-start.2
  14.8 5.4 %copy-start.4 = (s32[4]{0:T(128)S(1)}, s32[4]{0:T(128)}, u32[]{:S(2)}) copy-start(s32[4]{0:T(128)} %param.14) | copy-start | bytes 52
  14.8 6.0 %copy-start.5 = (s32[4,8]{1,0:T(4,128)S(1)}, s32[4,8]{1,0:T(4,128)}, u32[]{:S(2)}) copy-start(s32[4,8]{1,0:T(4,128)} %param.15) | copy-start | bytes 388
  14.8 43.3 %all-to-all-start = ((bf16[8,3,256,256]{3,2,1,0:T(8,128)(2,1)}), bf16[8,3,256,256]{3,2,1,0:T(8,128)(2,1)}, u32[]{:S(2)}, u32[]{:S(2)}) async-start(bf16[8,3,256,256]{3,2,1,0:T(8,128)(2,1)} %pad_maximum_fusion), calls=%async_computation | async-start | bytes 6291456 | tf_op jit(solution)/shard_map/all_to_all | solution.py:127
  20.1 178.0 %reduce-scatter.3.cloned.1.call-start = ((), (), s32[]{:S(2)}) async-start(), calls=%async_computation.6 | async-start | bytes 6553600 | tf_op jit(solution)/shard_map/reduce_scatter | solution.py:144
  106.3 41.4 %all-to-all-start.2 = ((bf16[8,3,256,256]{3,2,1,0:T(8,128)(2,1)}), bf16[8,3,256,256]{3,2,1,0:T(8,128)(2,1)S(1)}, u32[]{:S(2)}, u32[]{:S(2)}) async-start(bf16[8,3,256,256]{3,2,1,0:T(8,128)(2,1)} %pad_maximum_fusion.1), calls=%async_computation.3 | async-start | bytes 6291456 | tf_op jit(solution)/shard_map/all_to_all | solution.py:127
  110.0 184.8 %reduce-scatter.5.cloned.1.call-start = ((), (), s32[]{:S(2)}) async-start(), calls=%async_computation.7 | async-start | bytes 6553600 | tf_op jit(solution)/shard_map/reduce_scatter | solution.py:144
  147.7 1.7 copy-start
Sparse Core Ops, SparseCore 0:
  104.3 93.7 reduce-scatter.2
  200.4 94.3 reduce-scatter.4
